TPU v7x, 256 devices: a whole 4x4x8 slice. The times are simulated.
256 devices in a mesh: gx: 8 (over x, core), gy: 32 (over y, z).
Axes of the slice: x: 4, y: 4, z: 8, core: 2. Of those that a mesh axis runs over, the one named last changes fastest.
Arguments:
- fields: bfloat16 [672, 672, 1536], P('gx', 'gy'), may hold values from -16 to 16
- x_factor: bfloat16 [672, 336], replicated, may hold values from -0.00030517578 to 0.00030517578
- running_r: float32 [672, 672], replicated, as said below
Outputs:
- new_r: float32 [672, 672], P('gy', 'gx')
Inputs may be any that keep to these rules, and one draw needn't show every extreme that they name: `running_r`: upper triangular with a positive diagonal.
All inputs are finite; a program needn't handle non-finite values.
Results may differ from a plain program's by a relative error of at most 0.0003.
Values may be sent and summed in bfloat16 or wider, within the bound.
A program may use at most 256 MiB of HBM per device.

v0:
```python
import jax
import jax.numpy as jnp
from jax import lax
from jax.sharding import PartitionSpec as P


def fibre_gram(fibres):
    local_gram = lax.dot_general(
        fibres, fibres, (((0, 2), (0, 2)), ((), ())), preferred_element_type=jnp.float32
    )
    return lax.psum(local_gram, ("gx", "gy"))


def project_local(x_factor, block):
    full_x = block.shape[0]
    middle = block.shape[1]
    part_cells = block.shape[2]
    product = lax.dot_general(
        x_factor,
        block.reshape(full_x, middle * part_cells),
        (((0,), (0,)), ((), ())),
        preferred_element_type=jnp.float32,
    )
    return product.astype(jnp.bfloat16).reshape(x_factor.shape[1], middle, part_cells)


def on_device(fields, x_factor, running_r):
    full_y = running_r.shape[0]
    exchanged = lax.all_to_all(fields, "gx", split_axis=2, concat_axis=0, tiled=True)
    projected = project_local(x_factor, exchanged)
    fibres = lax.all_to_all(projected, "gy", split_axis=2, concat_axis=1, tiled=True)
    gram_sum = fibre_gram(fibres)
    total = (
        jnp.dot(
            running_r.T,
            running_r,
            precision=lax.Precision.HIGHEST,
            preferred_element_type=jnp.float32,
        )
        + gram_sum
    )
    upper_r = jnp.linalg.cholesky(total).T
    row_block = full_y // lax.axis_size("gy")
    col_block = full_y // lax.axis_size("gx")
    return lax.dynamic_slice(
        upper_r,
        (lax.axis_index("gy") * row_block, lax.axis_index("gx") * col_block),
        (row_block, col_block),
    )


def solution(mesh):
    in_specs = (P("gx", "gy", None), P(), P())
    out_specs = P("gy", "gx")
    return jax.shard_map(
        on_device, mesh=mesh, in_specs=in_specs, out_specs=out_specs, check_vma=False
    )
```

profile of v0, /device:TPU:2, one launch (start us, length us, event | category | flops | bytes accessed | tf_op | source)
XLA Modules:
  0.0 698.8 jit_solution(13633956588699801760)
XLA Ops:
  6.5 11.8 %copy.19 = bf16[84,21,1536]{0,1,2:T(8,128)(2,1)} copy(bf16[84,21,1536]{2,0,1:T(8,128)(2,1)} %param.3) | data formatting | bytes 10838016 | tf_op args[0]
  18.4 114.1 %all_to_all.33 = bf16[84,21,1536]{0,1,2:T(8,128)(2,1)} all-to-all(bf16[84,21,1536]{0,1,2:T(8,128)(2,1)} %copy.19), channel_id=1, replica_groups=mesh['gx'=8,'gy'=32] {'gx'}, dimensions={2} | all-to-all | bytes 10838016 | tf_op jit(solution)/shard_map/all_to_all | solution.py:29
  132.5 15.4 %copy.20 = bf16[84,21,8,192]{3,1,0,2:T(8,128)(2,1)} copy(bf16[84,21,8,192]{0,1,3,2:T(8,128)(2,1)} %bitcast.50) | data formatting | bytes 10838016 | tf_op jit(solution)/shard_map/all_to_all | solution.py:29
  147.9 12.5 %reshape.46 = bf16[672,4032]{1,0:T(8,128)(2,1)} reshape(bf16[8,84,21,192]{3,2,1,0:T(8,128)(2,1)} %bitcast.51) | data formatting | bytes 10838016 | tf_op jit(solution)/shard_map/reshape | solution.py:20
  160.4 6.4 convolution_convert_fusion
  166.8 4.5 copy.21
  171.3 3.7 copy.22
  175.1 91.4 %all_to_all.34 = bf16[336,21,192]{0,1,2:T(8,128)(2,1)S(1)} all-to-all(bf16[336,21,192]{0,1,2:T(8,128)(2,1)S(1)} %copy.22), channel_id=1, replica_groups=mesh['gx'=8,'gy'=32] {'gy'}, dimensions={2} | all-to-all | bytes 5419008 | tf_op jit(solution)/shard_map/all_to_all | solution.py:31
  266.5 2.2 copy.23
  268.7 6.0 all_to_all.30
  274.7 6.8 convolution_bitcast_fusion
  281.5 257.3 %all-reduce.3.cloned.1.call-done = f32[672,672]{0,1:T(8,128)} async-done(((f32[672,672]{0,1:T(8,128)}), f32[672,672]{0,1:T(8,128)}) %all-reduce.3.cloned.1.call-update) | async-done | bytes 1806352 | tf_op jit(solution)/shard_map/psum | solution.py:11
  538.8 8.2 %convolution_add_fusion = f32[672,672]{0,1:T(8,128)} fusion(f32[672,672]{0,1:T(8,128)} %all-reduce.3.cloned.1.call-done, f32[672,672]{1,0:T(8,128)S(1)} %copy-done), kind=kOutput, calls=%fused_computation.4 | convolution fusion | flops 3642024960 | bytes 5419008 | tf_op jit(solution)/shard_map/dot_general | solution.py:34
  547.0 3.1 copy.27
  550.2 2.5 fusion
  552.7 1.3 copy-done.1
  554.0 11.7 %cholesky.166 = f32[128,128]{1,0:T(8,128)S(1)} custom-call(f32[128,128]{1,0:T(8,128)S(1)} %cholesky.430), custom_call_target="Cholesky" | custom-call | tf_op jit(solution)/shard_map/jit(cholesky)/cholesky | solution.py:42
  565.7 9.8 %custom-call.43 = f32[1,128,128]{1,2,0:T(8,128)S(1)} custom-call(f32[1,128,128]{2,1,0:T(8,128)S(1)} %get-tuple-element.18), custom_call_target="InvertDiagBlocksLowerTriangular" | custom-call | tf_op jit(solution)/shard_map/jit(cholesky)/cholesky | solution.py:42
  575.6 1.4 cholesky.342
  577.0 2.1 constant_dynamic-update-slice_fusion.4
  579.0 1.3 convolution_subtract_fusion
  580.4 11.7 %cholesky.189 = f32[128,128]{1,0:T(8,128)S(1)} custom-call(f32[128,128]{1,0:T(8,128)S(1)} %cholesky.434), custom_call_target="Cholesky" | custom-call | tf_op jit(solution)/shard_map/jit(cholesky)/cholesky | solution.py:42
  592.1 0.7 select_reduce_fusion.3
  592.8 10.2 %custom-call.44 = f32[1,128,128]{1,2,0:T(8,128)S(1)} custom-call(f32[1,128,128]{2,1,0:T(8,128)S(1)} %get-tuple-element.15), custom_call_target="InvertDiagBlocksLowerTriangular" | custom-call | tf_op jit(solution)/shard_map/jit(cholesky)/cholesky | solution.py:42
  603.0 1.0 convolution_dynamic-update-slice_fusion
  604.0 1.6 convolution_subtract_fusion.1
  605.6 11.7 %cholesky.356 = f32[128,128]{1,0:T(8,128)S(1)} custom-call(f32[128,128]{1,0:T(8,128)S(1)} %cholesky.439), custom_call_target="Cholesky" | custom-call | tf_op jit(solution)/shard_map/jit(cholesky)/cholesky | solution.py:42
  618.0 0.7 compare_reduce_fusion.3
  618.7 9.8 %custom-call.45 = f32[1,128,128]{1,2,0:T(8,128)S(1)} custom-call(f32[1,128,128]{2,1,0:T(8,128)S(1)} %get-tuple-element.12), custom_call_target="InvertDiagBlocksLowerTriangular" | custom-call | tf_op jit(solution)/shard_map/jit(cholesky)/cholesky | solution.py:42
  628.5 1.0 convolution_dynamic-update-slice_fusion.1
  629.4 1.7 convolution_subtract_fusion.2
  631.1 11.8 %cholesky.375 = f32[128,128]{1,0:T(8,128)S(1)} custom-call(f32[128,128]{1,0:T(8,128)S(1)} %cholesky.444), custom_call_target="Cholesky" | custom-call | tf_op jit(solution)/shard_map/jit(cholesky)/cholesky | solution.py:42
  643.0 0.6 select_reduce_fusion.1
  643.6 0.7 compare_reduce_fusion.2
  644.3 9.8 %custom-call.46 = f32[1,128,128]{1,2,0:T(8,128)S(1)} custom-call(f32[1,128,128]{2,1,0:T(8,128)S(1)} %get-tuple-element.9), custom_call_target="InvertDiagBlocksLowerTriangular" | custom-call | tf_op jit(solution)/shard_map/jit(cholesky)/cholesky | solution.py:42
  654.1 0.9 convolution_dynamic-update-slice_fusion.2
  655.0 1.5 convolution_subtract_fusion.3
  656.5 11.7 %cholesky.394 = f32[128,128]{1,0:T(8,128)S(1)} custom-call(f32[128,128]{1,0:T(8,128)S(1)} %cholesky.449), custom_call_target="Cholesky" | custom-call | tf_op jit(solution)/shard_map/jit(cholesky)/cholesky | solution.py:42
  668.2 0.6 select_reduce_fusion
  668.9 0.7 compare_reduce_fusion.1
  669.5 9.8 %custom-call.47 = f32[1,128,128]{1,2,0:T(8,128)S(1)} custom-call(f32[1,128,128]{2,1,0:T(8,128)S(1)} %get-tuple-element.6), custom_call_target="InvertDiagBlocksLowerTriangular" | custom-call | tf_op jit(solution)/shard_map/jit(cholesky)/cholesky | solution.py:42
  679.3 0.8 convolution_dynamic-update-slice_fusion.3
  680.1 1.2 convolution_subtract_fusion.4
  681.3 2.9 cholesky.415
  684.8 0.7 compare_reduce_fusion
  685.6 0.6 compare_reduce_fusion.4
  690.0 1.0 fusion.20
  691.0 0.7 copy.28
  (15 shorter events, 1.3 us)
Async XLA Ops:
  6.5 532.3 %copy-start = (f32[672,672]{1,0:T(8,128)S(1)}, f32[672,672]{1,0:T(8,128)}, u32[]{:S(2)}) copy-start(f32[672,672]{1,0:T(8,128)} %param.5) | copy-start | bytes 5419012
  6.5 532.3 %all-reduce.3.cloned.1.call-start = ((), (), s32[]{:S(2)}) async-start(), calls=%async_computation.2 | async-start | bytes 4128768 | tf_op jit(solution)/shard_map/psum | solution.py:11
  147.9 12.5 %copy-start.2 = (bf16[672,336]{1,0:T(8,128)(2,1)S(1)}, bf16[672,336]{1,0:T(8,128)(2,1)}, u32[]{:S(2)}) copy-start(bf16[672,336]{1,0:T(8,128)(2,1)} %param.4) | copy-start | bytes 1354756
  552.6 1.3 copy-start.1
Sparse Core Ops, SparseCore 0:
  281.6 257.1 all-reduce.2
where the time goes:
time: 706 us; the launch traced here: 699 us
  waiting for transfers between devices  257 us (36%)
  blocking collectives  206 us (29%)
  other arithmetic  121 us (17%)
  local copies, waits for them, and re-layouts  62.8 us (9%)
  matrix products  34.5 us (5%)
  between operations  17.6 us (2%)
    psum x1, waiting for transfers between devices, fibre_gram(): return lax.psum(local_gram, ('gx', 'gy'))  257 us
    another operation x22, other arithmetic, on_device(): upper_r = jnp.linalg.cholesky(total).T  118 us
    all_to_all x1, blocking collectives, on_device(): lax.all_to_all(fields, 'gx', split_axis=2, concat_axis=0, tiled=True)  114 us
    all_to_all x1, blocking collectives, on_device(): lax.all_to_all(projected, 'gy', split_axis=2, concat_axis=1, tiled=True)  91.4 us
    all_to_all x1, local copies, waits for them, and re-layouts, on_device(): lax.all_to_all(fields, 'gx', split_axis=2, concat_axis=0, tiled=True)  15.4 us
  transfers between devices with their start and end apart: 1, of which 1 were waited for; matrix products, arithmetic and copies ran while one was open for 0% of the time, Pallas kernels for 0%

commit v1 on v0

--- a/solution.py
+++ b/solution.py
@@ -8,7 +8,7 @@
     local_gram = lax.dot_general(
         fibres, fibres, (((0, 2), (0, 2)), ((), ())), preferred_element_type=jnp.float32
     )
-    return lax.psum(local_gram, ("gx", "gy"))
+    return jax.lax.psum(jax.lax.psum(local_gram, axis_name="gy"), axis_name="gx")
 
 
 def project_local(x_factor, block):

time: 706 us -> 669 us (0.948)
  waiting for transfers between devices: 257 us -> 217 us
    psum x1 -> x2, waiting for transfers between devices: 257 us -> 217 us  [the longest x1 149 us: fibre_gram(): jax.lax.psum(local_gram, axis_name='gy')]
  transfers between devices with their start and end apart: 1 -> 2, of which waited for: 1 -> 2; matrix products, arithmetic and copies ran while one was open for 0% -> 0% of each run, Pallas kernels for 0% -> 0%
where the time goes in v1:
time: 669 us; the launch traced here: 659 us
  waiting for transfers between devices  217 us (32%)
  blocking collectives  205 us (31%)
  other arithmetic  121 us (18%)
  local copies, waits for them, and re-layouts  62.7 us (9%)
  matrix products  34.5 us (5%)
  between operations  17.6 us (3%)
    psum x1, waiting for transfers between devices, fibre_gram(): jax.lax.psum(local_gram, axis_name='gy')  149 us
    another operation x22, other arithmetic, on_device(): upper_r = jnp.linalg.cholesky(total).T  118 us
    all_to_all x1, blocking collectives, on_device(): lax.all_to_all(fields, 'gx', split_axis=2, concat_axis=0, tiled=True)  114 us
    all_to_all x1, blocking collectives, on_device(): lax.all_to_all(projected, 'gy', split_axis=2, concat_axis=1, tiled=True)  91.2 us
    psum x1, waiting for transfers between devices, fibre_gram(): jax.lax.psum(jax.lax.psum(local_gram, axis_name='gy'), axis_name='gx')  68.2 us
    all_to_all x1, local copies, waits for them, and re-layouts, on_device(): lax.all_to_all(fields, 'gx', split_axis=2, concat_axis=0, tiled=True)  15.4 us
  transfers between devices with their start and end apart: 2, of which 2 were waited for; matrix products, arithmetic and copies ran while one was open for 0% of the time, Pallas kernels for 0%

profile of v1, /device:TPU:2, one launch (start us, length us, event | category | flops | bytes accessed | tf_op | source)
XLA Modules:
  0.0 658.6 jit_solution(6730911013338022619)
XLA Ops:
  6.5 11.8 %copy.19 = bf16[84,21,1536]{0,1,2:T(8,128)(2,1)} copy(bf16[84,21,1536]{2,0,1:T(8,128)(2,1)} %param.3) | data formatting | bytes 10838016 | tf_op args[0]
  18.4 114.1 %all_to_all.33 = bf16[84,21,1536]{0,1,2:T(8,128)(2,1)} all-to-all(bf16[84,21,1536]{0,1,2:T(8,128)(2,1)} %copy.19), channel_id=1, replica_groups=mesh['gx'=8,'gy'=32] {'gx'}, dimensions={2} | all-to-all | bytes 10838016 | tf_op jit(solution)/shard_map/all_to_all | solution.py:29
  132.5 15.4 %copy.20 = bf16[84,21,8,192]{3,1,0,2:T(8,128)(2,1)} copy(bf16[84,21,8,192]{0,1,3,2:T(8,128)(2,1)} %bitcast.50) | data formatting | bytes 10838016 | tf_op jit(solution)/shard_map/all_to_all | solution.py:29
  147.9 12.5 %reshape.46 = bf16[672,4032]{1,0:T(8,128)(2,1)} reshape(bf16[8,84,21,192]{3,2,1,0:T(8,128)(2,1)} %bitcast.51) | data formatting | bytes 10838016 | tf_op jit(solution)/shard_map/reshape | solution.py:20
  160.4 6.4 convolution_convert_fusion
  166.8 4.5 copy.21
  171.3 3.7 copy.22
  175.1 91.2 %all_to_all.34 = bf16[336,21,192]{0,1,2:T(8,128)(2,1)S(1)} all-to-all(bf16[336,21,192]{0,1,2:T(8,128)(2,1)S(1)} %copy.22), channel_id=1, replica_groups=mesh['gx'=8,'gy'=32] {'gy'}, dimensions={2} | all-to-all | bytes 5419008 | tf_op jit(solution)/shard_map/all_to_all | solution.py:31
  266.3 2.2 copy.23
  268.5 6.0 all_to_all.30
  274.5 6.8 %convolution_bitcast_fusion = f32[672,672]{0,1:T(8,128)} fusion(bf16[336,672,6]{0,1,2:T(8,128)(2,1)} %all_to_all.30), kind=kOutput, calls=%fused_computation.3 | convolution fusion | flops 1820786688 | bytes 4515840 | tf_op jit(solution)/shard_map/dot_general | solution.py:8
  281.6 148.9 %all-reduce.4.cloned.1.call-done = f32[672,672]{0,1:T(8,128)} async-done(((f32[672,672]{0,1:T(8,128)}), f32[672,672]{0,1:T(8,128)}) %all-reduce.4.cloned.1.call-update) | async-done | bytes 1806352 | tf_op jit(solution)/shard_map/psum | solution.py:11
  430.5 68.2 %all-reduce.6.cloned.1.call-done = f32[672,672]{0,1:T(8,128)} async-done(((f32[672,672]{0,1:T(8,128)}), f32[672,672]{0,1:T(8,128)}) %all-reduce.6.cloned.1.call-update) | async-done | bytes 1806352 | tf_op jit(solution)/shard_map/psum | solution.py:11
  498.7 8.3 %convolution_add_fusion = f32[672,672]{0,1:T(8,128)} fusion(f32[672,672]{0,1:T(8,128)} %all-reduce.6.cloned.1.call-done, f32[672,672]{1,0:T(8,128)S(1)} %copy-done), kind=kOutput, calls=%fused_computation.4 | convolution fusion | flops 3642024960 | bytes 5419008 | tf_op jit(solution)/shard_map/dot_general | solution.py:34
  507.0 3.1 copy.27
  510.1 2.5 fusion
  512.6 1.3 copy-done.1
  513.9 11.7 %cholesky.166 = f32[128,128]{1,0:T(8,128)S(1)} custom-call(f32[128,128]{1,0:T(8,128)S(1)} %cholesky.430), custom_call_target="Cholesky" | custom-call | tf_op jit(solution)/shard_map/jit(cholesky)/cholesky | solution.py:42
  525.6 9.8 %custom-call.43 = f32[1,128,128]{1,2,0:T(8,128)S(1)} custom-call(f32[1,128,128]{2,1,0:T(8,128)S(1)} %get-tuple-element.18), custom_call_target="InvertDiagBlocksLowerTriangular" | custom-call | tf_op jit(solution)/shard_map/jit(cholesky)/cholesky | solution.py:42
  535.5 1.4 cholesky.342
  536.9 2.1 constant_dynamic-update-slice_fusion.4
  538.9 1.3 convolution_subtract_fusion
  540.3 11.7 %cholesky.189 = f32[128,128]{1,0:T(8,128)S(1)} custom-call(f32[128,128]{1,0:T(8,128)S(1)} %cholesky.434), custom_call_target="Cholesky" | custom-call | tf_op jit(solution)/shard_map/jit(cholesky)/cholesky | solution.py:42
  552.0 0.7 select_reduce_fusion.3
  552.7 10.2 %custom-call.44 = f32[1,128,128]{1,2,0:T(8,128)S(1)} custom-call(f32[1,128,128]{2,1,0:T(8,128)S(1)} %get-tuple-element.15), custom_call_target="InvertDiagBlocksLowerTriangular" | custom-call | tf_op jit(solution)/shard_map/jit(cholesky)/cholesky | solution.py:42
  562.9 1.0 convolution_dynamic-update-slice_fusion
  563.9 1.6 convolution_subtract_fusion.1
  565.5 11.7 %cholesky.356 = f32[128,128]{1,0:T(8,128)S(1)} custom-call(f32[128,128]{1,0:T(8,128)S(1)} %cholesky.439), custom_call_target="Cholesky" | custom-call | tf_op jit(solution)/shard_map/jit(cholesky)/cholesky | solution.py:42
  577.9 0.7 compare_reduce_fusion.3
  578.6 9.8 %custom-call.45 = f32[1,128,128]{1,2,0:T(8,128)S(1)} custom-call(f32[1,128,128]{2,1,0:T(8,128)S(1)} %get-tuple-element.12), custom_call_target="InvertDiagBlocksLowerTriangular" | custom-call | tf_op jit(solution)/shard_map/jit(cholesky)/cholesky | solution.py:42
  588.4 0.9 convolution_dynamic-update-slice_fusion.1
  589.3 1.7 convolution_subtract_fusion.2
  591.0 11.8 %cholesky.375 = f32[128,128]{1,0:T(8,128)S(1)} custom-call(f32[128,128]{1,0:T(8,128)S(1)} %cholesky.444), custom_call_target="Cholesky" | custom-call | tf_op jit(solution)/shard_map/jit(cholesky)/cholesky | solution.py:42
  602.9 0.6 select_reduce_fusion.1
  603.5 0.7 compare_reduce_fusion.2
  604.2 9.8 %custom-call.46 = f32[1,128,128]{1,2,0:T(8,128)S(1)} custom-call(f32[1,128,128]{2,1,0:T(8,128)S(1)} %get-tuple-element.9), custom_call_target="InvertDiagBlocksLowerTriangular" | custom-call | tf_op jit(solution)/shard_map/jit(cholesky)/cholesky | solution.py:42
  614.0 0.9 convolution_dynamic-update-slice_fusion.2
  614.9 1.5 convolution_subtract_fusion.3
  616.4 11.7 %cholesky.394 = f32[128,128]{1,0:T(8,128)S(1)} custom-call(f32[128,128]{1,0:T(8,128)S(1)} %cholesky.449), custom_call_target="Cholesky" | custom-call | tf_op jit(solution)/shard_map/jit(cholesky)/cholesky | solution.py:42
  628.1 0.6 select_reduce_fusion
  628.8 0.7 compare_reduce_fusion.1
  629.4 9.8 %custom-call.47 = f32[1,128,128]{1,2,0:T(8,128)S(1)} custom-call(f32[1,128,128]{2,1,0:T(8,128)S(1)} %get-tuple-element.6), custom_call_target="InvertDiagBlocksLowerTriangular" | custom-call | tf_op jit(solution)/shard_map/jit(cholesky)/cholesky | solution.py:42
  639.2 0.8 convolution_dynamic-update-slice_fusion.3
  640.0 1.2 convolution_subtract_fusion.4
  641.2 2.9 cholesky.415
  644.7 0.7 compare_reduce_fusion
  649.9 1.0 fusion.20
  650.9 0.7 copy.28
  (18 shorter events, 2.2 us)
Async XLA Ops:
  6.5 492.2 %copy-start = (f32[672,672]{1,0:T(8,128)S(1)}, f32[672,672]{1,0:T(8,128)}, u32[]{:S(2)}) copy-start(f32[672,672]{1,0:T(8,128)} %param.5) | copy-start | bytes 5419012
  6.5 423.9 %all-reduce.4.cloned.1.call-start = ((), (), s32[]{:S(2)}) async-start(), calls=%async_computation.2 | async-start | bytes 4128768 | tf_op jit(solution)/shard_map/psum | solution.py:11
  147.9 12.5 %copy-start.2 = (bf16[672,336]{1,0:T(8,128)(2,1)S(1)}, bf16[672,336]{1,0:T(8,128)(2,1)}, u32[]{:S(2)}) copy-start(bf16[672,336]{1,0:T(8,128)(2,1)} %param.4) | copy-start | bytes 1354756
  281.3 217.4 %all-reduce.6.cloned.1.call-start = ((), (), s32[]{:S(2)}) async-start(), calls=%async_computation.3 | async-start | bytes 4128768 | tf_op jit(solution)/shard_map/psum | solution.py:11
  512.6 1.3 copy-start.1
Sparse Core Ops, SparseCore 0:
  281.5 148.9 all-reduce.3
  432.8 65.8 all-reduce.5
